TPU v7x, 32 devices: a whole 2x2x4 slice. The times are simulated.
32 devices in a mesh: scene: 2 (over y), tok: 8 (over z, x), hid: 2 (over core).
Axes of the slice: x: 2, y: 2, z: 4, core: 2. Of those that a mesh axis runs over, the one named last changes fastest.
Arguments:
- input_keys: bfloat16 [16384, 384], P(('scene', 'tok'), 'hid'), parts along dimension 0, may hold values from -6 to 6
- input_values: bfloat16 [16384, 384], P(('scene', 'tok'), 'hid'), parts along dimension 0, may hold values from -6 to 6
- input_lr: float32 [16384], P(('scene', 'tok')), parts along dimension 0, may hold values from 0.1 to 1
- gate_weight: bfloat16 [384, 1536], P('tok', 'hid'), may hold values from -0.3125 to 0.3125
- up_weight: bfloat16 [384, 1536], P('tok', 'hid'), may hold values from -0.3125 to 0.3125
- down_weight: bfloat16 [384, 1536], P('tok', 'hid'), may hold values from -0.15625 to 0.15625
- queries: bfloat16 [2048, 384], P(('scene', 'tok'), 'hid'), parts along dimension 0, may hold values from -6 to 6
- out_grad: bfloat16 [2048, 384], P(('scene', 'tok'), 'hid'), parts along dimension 0, may hold values from -6 to 6
Outputs:
- target_out: bfloat16 [2048, 384], P(('scene', 'tok'), 'hid'), parts along dimension 0
- query_grad: bfloat16 [2048, 384], P(('scene', 'tok'), 'hid'), parts along dimension 0
There are 2 independent parts, one for each index of `scene`. A program takes and returns all parts, laid end to end along the dimension named above; an argument that names none is the same for every part. Nothing has to cross between parts.
All inputs are finite; a program needn't handle non-finite values.
Results may differ from a plain program's by a relative error of at most 0.009.
Values may be sent and summed in bfloat16 or wider, within the bound.
A program may use at most 64 MiB of HBM per device.

v0:
```python
import jax
import jax.numpy as jnp
from jax import lax
from jax.sharding import PartitionSpec as P

HID = 1536
step_ratio = 0.5
epsilon = 1e-06


def silu_slope(pre):
    sigma = jax.nn.sigmoid(pre)
    return sigma * (1.0 + pre * (1.0 - sigma))


def contract_rows(left, right):
    return lax.dot_general(
        left, right, (((0,), (0,)), ((), ())), preferred_element_type=jnp.float32
    )


def contract_cols(left, right):
    return lax.dot_general(
        left, right, (((1,), (1,)), ((), ())), preferred_element_type=jnp.float32
    )


def finish(moved, wsq, msq):
    return (moved * (jnp.sqrt(wsq) / jnp.sqrt(msq + epsilon))[:, None]).astype(jnp.bfloat16)


def shards(
    input_keys, input_values, input_lr, gate_weight, up_weight, down_weight, queries, out_grad
):
    keys, values = (
        lax.all_gather(input_keys, "hid", axis=1, tiled=True),
        lax.all_gather(input_values, "hid", axis=1, tiled=True),
    )
    w_gate, w_up, w_down = (
        lax.all_gather(gate_weight, "tok", axis=0, tiled=True),
        lax.all_gather(up_weight, "tok", axis=0, tiled=True),
        lax.all_gather(down_weight, "tok", axis=0, tiled=True),
    )
    scaled = (input_lr[:, None] * values.astype(jnp.float32)).astype(jnp.bfloat16)
    key_gate = jnp.dot(keys, w_gate, preferred_element_type=jnp.float32)
    key_up = jnp.dot(keys, w_up, preferred_element_type=jnp.float32)
    gate_act = jax.nn.silu(key_gate)
    key_act = (gate_act * key_up).astype(jnp.bfloat16)
    back = jnp.dot(scaled, w_down, preferred_element_type=jnp.float32)
    d_gate = (-back * key_up * silu_slope(key_gate)).astype(jnp.bfloat16)
    d_up = (-back * gate_act).astype(jnp.bfloat16)
    width = gate_weight.shape[1]
    grads = lax.psum(
        jnp.concatenate(
            [
                contract_rows(keys, d_gate),
                contract_rows(keys, d_up),
                -contract_rows(scaled, key_act),
            ],
            axis=1,
        ),
        "tok",
    )
    olds = (w_gate, w_up, w_down)
    pieces = [grads[:, :width], grads[:, width : 2 * width], grads[:, 2 * width :]]
    weights = [old.astype(jnp.float32) for old in olds]
    renewed = []
    stats = []
    for weight, grad in zip(weights, pieces):
        stats.append(jnp.sum(weight * weight, axis=1))
        stats.append(jnp.sum(weight * grad, axis=1))
        stats.append(jnp.sum(grad * grad, axis=1))
    totals = lax.psum(
        (stats[0], stats[1], stats[2], stats[3], stats[4], stats[5], stats[6], stats[7], stats[8]),
        "hid",
    )
    for index in range(3):
        wsq = totals[3 * index] / HID
        cross = totals[3 * index + 1] / HID
        gsq = totals[3 * index + 2] / HID
        scale = step_ratio * jnp.sqrt(wsq) / jnp.sqrt(gsq + epsilon)
        moved = weights[index] - scale[:, None] * pieces[index]
        msq = wsq - 2.0 * scale * cross + scale * scale * gsq
        renewed.append(finish(moved, wsq, msq))
    new_gate, new_up, new_down = (renewed[0], renewed[1], renewed[2])
    query_rows, grad_rows = (
        lax.all_gather(queries, "hid", axis=1, tiled=True),
        lax.all_gather(out_grad, "hid", axis=1, tiled=True),
    )
    query_gate = jnp.dot(query_rows, new_gate, preferred_element_type=jnp.float32)
    query_up = jnp.dot(query_rows, new_up, preferred_element_type=jnp.float32)
    query_silu = jax.nn.silu(query_gate)
    query_act = (query_silu * query_up).astype(jnp.bfloat16)
    out_part = contract_cols(query_act, new_down)
    query_back = jnp.dot(grad_rows, new_down, preferred_element_type=jnp.float32)
    q_gate_grad = (query_back * query_up * silu_slope(query_gate)).astype(jnp.bfloat16)
    q_up_grad = (query_back * query_silu).astype(jnp.bfloat16)
    grad_part = contract_cols(q_gate_grad, new_gate) + contract_cols(q_up_grad, new_up)
    out_sum, grad_sum = (
        lax.psum_scatter(
            out_part.astype(jnp.bfloat16), "hid", scatter_dimension=1, tiled=True
        ).astype(jnp.float32),
        lax.psum_scatter(
            grad_part.astype(jnp.bfloat16), "hid", scatter_dimension=1, tiled=True
        ).astype(jnp.float32),
    )
    return (out_sum.astype(jnp.bfloat16), grad_sum.astype(jnp.bfloat16))


def solution(mesh):
    return jax.shard_map(
        shards,
        mesh=mesh,
        in_specs=(
            P(("scene", "tok"), "hid"),
            P(("scene", "tok"), "hid"),
            P(("scene", "tok")),
            P("tok", "hid"),
            P("tok", "hid"),
            P("tok", "hid"),
            P(("scene", "tok"), "hid"),
            P(("scene", "tok"), "hid"),
        ),
        out_specs=(P(("scene", "tok"), "hid"), P(("scene", "tok"), "hid")),
        check_vma=False,
    )
```

profile of v0, /device:TPU:0, one launch (start us, length us, event | category | flops | bytes accessed | tf_op | source)
XLA Modules:
  0.0 297.7 jit_solution(15559393787212214560)
XLA Ops:
  7.2 0.0 copy-start.6
  7.2 0.0 all-reduce.3.cloned.1.call-start
  7.2 2.7 all_gather.24
  9.9 33.4 %all_gather.21 = bf16[384,768]{1,0:T(8,128)(2,1)S(1)} all-gather(bf16[48,768]{1,0:T(8,128)(2,1)} %param.11), channel_id=1, replica_groups=mesh['scene'=2,'tok'=8,'hid'=2] {'tok'}, dimensions={0}, use_global_device_ids=true | all-gather | bytes 663552 | tf_op jit(solution)/shard_map/all_gather | solution.py:40
  43.4 31.3 %all_gather.25 = bf16[384,768]{1,0:T(8,128)(2,1)S(1)} all-gather(bf16[48,768]{1,0:T(8,128)(2,1)S(1)} %copy-done.6), channel_id=1, replica_groups=mesh['scene'=2,'tok'=8,'hid'=2] {'tok'}, dimensions={0}, use_global_device_ids=true | all-gather | bytes 663552 | tf_op jit(solution)/shard_map/all_gather | solution.py:41
  74.6 1.0 fusion.34
  75.7 0.0 copy-start.5
  75.7 0.0 copy-start.7
  75.7 1.0 fusion.33
  76.7 0.0 copy-start.10
  76.7 2.4 all_gather.22
  79.1 31.4 %all_gather.23 = bf16[384,768]{1,0:T(8,128)(2,1)S(1)} all-gather(bf16[48,768]{1,0:T(8,128)(2,1)S(1)} %copy-done.7), channel_id=1, replica_groups=mesh['scene'=2,'tok'=8,'hid'=2] {'tok'}, dimensions={0}, use_global_device_ids=true | all-gather | bytes 663552 | tf_op jit(solution)/shard_map/all_gather | solution.py:42
  110.5 1.0 fusion.20
  111.6 1.2 fusion.6
  112.8 1.5 fusion.4
  114.3 1.3 fusion.5
  115.6 2.0 pad_maximum_fusion
  117.6 0.0 all-reduce.3.cloned.1.call-update
  117.7 0.0 copy-start.8
  117.7 0.0 copy-start.9
  117.7 0.0 reduce-scatter.5.cloned.1.call-start
  117.7 1.1 copy.14
  118.8 1.1 copy.16
  119.8 1.1 copy.17
  121.0 2.0 all_gather.27
  123.0 2.0 all_gather.26
  125.0 132.9 %all-reduce.3.cloned.1.call-done = f32[384,2304]{0,1:T(8,128)} async-done(((f32[384,2304]{0,1:T(8,128)}), f32[384,2304]{0,1:T(8,128)}) %all-reduce.3.cloned.1.call-update) | async-done | bytes 3538960 | tf_op jit(solution)/shard_map/psum | solution.py:53
  257.9 4.1 %multiply_reduce_fusion.2 = (f32[384]{0:T(512)S(1)}, f32[384]{0:T(512)S(1)}, f32[384]{0:T(512)S(1)}, f32[384]{0:T(512)S(1)}, f32[384]{0:T(512)}, /*index=5*/f32[...) fusion(f32[384,2304]{0,1:T(8,128)} %all-reduce.3.cloned.1.call-done, bf16[384,768]{0,1:T(8,128)(2,1)} %copy.14, ...), kind=kLoop, calls=%fused_computation.39 | loop fusion | flops 6189696 | bytes 5322240 | tf_op jit(solution)/shard_map/reduce_sum | solution.py:72
  261.9 4.6 %all-reduce = (f32[384]{0:T(512)}, f32[384]{0:T(512)}, f32[384]{0:T(512)}, f32[384]{0:T(512)}, f32[384]{0:T(512)}, /*index=5*/f32[384]{0:T(512)}, f32[384]{0:T(512)}, f32[384]{0:T(512)}, f32[384]{0:T(512)}) all-reduce(f32[384]{0:T(512)S(1)} %get-tuple-element.5, ...), channel_id=1, replica_groups=mesh['scene'=2,'tok'=8,'hid'=2] {'hid'}, use_global_device_ids=true, to_apply=%region_18.19 | all-reduce | flops 3456 | bytes 27648 | tf_op jit(solution)/shard_map/psum | solution.py:73
  266.5 0.7 rsqrt_multiply_fusion.5
  267.2 0.8 rsqrt_multiply_fusion.1
  268.0 0.0 copy-done
  268.0 0.0 copy-start.3
  268.0 2.0 fusion.9
  270.1 0.3 convolution_bitcast_fusion.1
  270.4 0.3 convolution_bitcast_fusion.2
  270.7 0.3 copy-done.4
  271.0 0.3 convolution_bitcast_fusion
  271.4 0.0 copy-done.1
  271.4 0.5 fusion.24
  271.8 1.1 fusion.19
  272.9 0.0 reduce-scatter.5.cloned.1.call-update
  272.9 0.0 reduce-scatter.3.cloned.1.call-start
  273.0 0.0 copy-done.2
  273.0 1.0 convolution_convert_fusion
  274.0 0.0 reduce-scatter.3.cloned.1.call-update
  274.0 5.6 %reduce-scatter.5.cloned.1.call-done = bf16[128,192]{0,1:T(8,128)(2,1)} async-done(((bf16[128,384]{0,1:T(8,128)(2,1)}), bf16[128,192]{0,1:T(8,128)(2,1)}) %reduce-scatter.5.cloned.1.call-update) | async-done | bytes 49168 | tf_op jit(solution)/shard_map/reduce_scatter | solution.py:103
  279.7 11.5 %reduce-scatter.3.cloned.1.call-done = bf16[128,192]{0,1:T(8,128)(2,1)} async-done(((bf16[128,384]{0,1:T(8,128)(2,1)}), bf16[128,192]{0,1:T(8,128)(2,1)}) %reduce-scatter.3.cloned.1.call-update) | async-done | bytes 49168 | tf_op jit(solution)/shard_map/reduce_scatter | solution.py:100
  (11 shorter events, 0.0 us)
Async XLA Ops:
  7.2 36.2 %copy-start.6 = (bf16[48,768]{1,0:T(8,128)(2,1)S(1)}, bf16[48,768]{1,0:T(8,128)(2,1)}, u32[]{:S(2)}) copy-start(bf16[48,768]{1,0:T(8,128)(2,1)} %param.12) | copy-start | bytes 221188
  7.2 250.7 %all-reduce.3.cloned.1.call-start = ((), (), s32[]{:S(2)}) async-start(), calls=%async_computation.2 | async-start | bytes 7077888 | tf_op jit(solution)/shard_map/psum | solution.py:53
  75.7 1.1 copy-start.5
  75.7 3.4 %copy-start.7 = (bf16[48,768]{1,0:T(8,128)(2,1)S(1)}, bf16[48,768]{1,0:T(8,128)(2,1)}, u32[]{:S(2)}) copy-start(bf16[48,768]{1,0:T(8,128)(2,1)} %param.13) | copy-start | bytes 221188
  76.7 33.8 %copy-start.10 = (f32[1024]{0:T(1024)S(1)}, f32[1024]{0:T(1024)}, u32[]{:S(2)}) copy-start(f32[1024]{0:T(1024)} %param.10) | copy-start | bytes 12292
  117.7 3.3 %copy-start.8 = (bf16[128,192]{0,1:T(8,128)(2,1)S(1)}, bf16[128,192]{0,1:T(8,128)(2,1)}, u32[]{:S(2)}) copy-start(bf16[128,192]{0,1:T(8,128)(2,1)} %param.15) | copy-start | bytes 147460
  117.7 5.3 %copy-start.9 = (bf16[128,192]{0,1:T(8,128)(2,1)S(1)}, bf16[128,192]{0,1:T(8,128)(2,1)}, u32[]{:S(2)}) copy-start(bf16[128,192]{0,1:T(8,128)(2,1)} %param.14) | copy-start | bytes 147460
  117.7 162.0 %reduce-scatter.5.cloned.1.call-start = ((), (), s32[]{:S(2)}) async-start(), calls=%async_computation.4 | async-start | bytes 147456 | tf_op jit(solution)/shard_map/reduce_scatter | solution.py:103
  257.8 10.2 %copy-start = (f32[384,2304]{0,1:T(8,128)S(1)}, f32[384,2304]{0,1:T(8,128)}, u32[]{:S(2)}) copy-start(f32[384,2304]{0,1:T(8,128)} %all-reduce.3.cloned.1.call-done) | copy-start | bytes 10616836
  268.0 2.1 copy-start.3
  270.0 1.3 copy-start.1
  270.1 1.0 copy-start.4
  271.8 1.2 copy-start.2
  272.9 18.2 %reduce-scatter.3.cloned.1.call-start = ((), (), s32[]{:S(2)}) async-start(), calls=%async_computation.3 | async-start | bytes 147456 | tf_op jit(solution)/shard_map/reduce_scatter | solution.py:100
Sparse Core Ops, SparseCore 0:
  117.8 140.0 all-reduce.2
  273.1 6.5 reduce-scatter.4
  282.5 8.6 reduce-scatter.2
where the time goes:
time: 298 us
  waiting for transfers between devices  150 us (50%)
  blocking collectives  110 us (37%)
  between operations  13.9 us (5%)
  matrix products  10.6 us (4%)
  other arithmetic  9.59 us (3%)
  local copies, waits for them, and re-layouts  3.61 us (1%)
    psum x1, waiting for transfers between devices, shards(): lax.psum(jnp.concatenate([contract_rows(keys, d_gate), contract_rows(keys...  133 us
    all_gather x1, blocking collectives, shards(): lax.all_gather(gate_weight, 'tok', axis=0, tiled=True)  33.4 us
    all_gather x1, blocking collectives, shards(): lax.all_gather(down_weight, 'tok', axis=0, tiled=True)  31.4 us
    all_gather x1, blocking collectives, shards(): lax.all_gather(up_weight, 'tok', axis=0, tiled=True)  31.3 us
    reduce_scatter x1, waiting for transfers between devices, shards(): lax.psum_scatter(out_part.astype(jnp.bfloat16), 'hid', scatter_dimension=...  11.5 us
  transfers between devices with their start and end apart: 3, of which 3 were waited for; matrix products, arithmetic and copies ran while one was open for 1% of the time, Pallas kernels for 0%

commit v1 on v0

--- a/solution.py
+++ b/solution.py
@@ -6,6 +6,22 @@
 HID = 1536
 step_ratio = 0.5
 epsilon = 1e-06
+
+
+def collect(x, axis, dim):
+    ways, here, step = (lax.axis_size(axis), lax.axis_index(axis), x.shape[dim])
+    lengths = [n * ways if d == dim else n for d, n in enumerate(x.shape)]
+    full = lax.dynamic_update_slice_in_dim(jnp.zeros(lengths, x.dtype), x, here * step, axis=dim)
+    going_up = going_down = x
+    for far in range(1, ways // 2 + 1):
+        going_up = lax.ppermute(going_up, axis, [(d, (d + 1) % ways) for d in range(ways)])
+        full = lax.dynamic_update_slice_in_dim(full, going_up, (here - far) % ways * step, axis=dim)
+        if 2 * far < ways:
+            going_down = lax.ppermute(going_down, axis, [(d, (d - 1) % ways) for d in range(ways)])
+            full = lax.dynamic_update_slice_in_dim(
+                full, going_down, (here + far) % ways * step, axis=dim
+            )
+    return full
 
 
 def silu_slope(pre):
@@ -38,7 +54,7 @@
     )
     w_gate, w_up, w_down = (
         lax.all_gather(gate_weight, "tok", axis=0, tiled=True),
-        lax.all_gather(up_weight, "tok", axis=0, tiled=True),
+        collect(up_weight, "tok", 0),
         lax.all_gather(down_weight, "tok", axis=0, tiled=True),
     )
     scaled = (input_lr[:, None] * values.astype(jnp.float32)).astype(jnp.bfloat16)

time: 298 us -> 318 us (1.067)
  blocking collectives: 110 us -> 77.1 us
  local copies, waits for them, and re-layouts: 3.61 us -> 31 us
  starting transfers between devices: 0.12 us -> 16.3 us
  waiting for transfers between devices: 150 us -> 155 us
    all_gather x1 -> x0, blocking collectives: 31.3 us -> none  [shards(): lax.all_gather(up_weight, 'tok', axis=0, tiled=True)]
    dynamic_update_slice x0 -> x8, local copies, waits for them, and re-layouts: none -> 26.3 us  [the longest x4 13.6 us: collect(): lax.dynamic_update_slice_in_dim(full, going_up, (here - far) % ways * ste...]
    ppermute x0 -> x7, starting transfers between devices: none -> 16.2 us  [the longest x3 13.2 us: collect(): lax.ppermute(going_down, axis, [(d, (d - 1) % ways) for d in range(ways)])]
    ppermute x0 -> x7, waiting for transfers between devices: none -> 3.42 us  [the longest x3 2.02 us: collect(): lax.ppermute(going_down, axis, [(d, (d - 1) % ways) for d in range(ways)])]
  transfers between devices with their start and end apart: 3 -> 10, of which waited for: 3 -> 5; matrix products, arithmetic and copies ran while one was open for 1% -> 10% of each run, Pallas kernels for 0% -> 0%
where the time goes in v1:
time: 318 us; the launch traced here: 317 us
  waiting for transfers between devices  155 us (49%)
  blocking collectives  77.1 us (24%)
  local copies, waits for them, and re-layouts  31 us (10%)
  starting transfers between devices  16.3 us (5%)
  between operations  14.2 us (4%)
  matrix products  13.7 us (4%)
  other arithmetic  9.62 us (3%)
    psum x1, waiting for transfers between devices, shards(): lax.psum(jnp.concatenate([contract_rows(keys, d_gate), contract_rows(keys...  134 us
    all_gather x1, blocking collectives, shards(): lax.all_gather(down_weight, 'tok', axis=0, tiled=True)  31.8 us
    all_gather x1, blocking collectives, shards(): lax.all_gather(gate_weight, 'tok', axis=0, tiled=True)  31.5 us
    dynamic_update_slice x4, local copies, waits for them, and re-layouts, collect(): lax.dynamic_update_slice_in_dim(full, going_up, (here - far) % ways * ste...  13.6 us
    ppermute x3, starting transfers between devices, collect(): lax.ppermute(going_down, axis, [(d, (d - 1) % ways) for d in range(ways)])  13.2 us
    reduce_scatter x1, waiting for transfers between devices, shards(): lax.psum_scatter(out_part.astype(jnp.bfloat16), 'hid', scatter_dimension=...  11.5 us
    dynamic_update_slice x3, local copies, waits for them, and re-layouts, collect(): lax.dynamic_update_slice_in_dim(full, going_down, (here + far) % ways * s...  10.6 us
    dot_general x3, matrix products, contract_rows(): lax.dot_general(left, right, (((0,), (0,)), ((), ())), preferred_element_...  7.17 us
  transfers between devices with their start and end apart: 10, of which 5 were waited for; matrix products, arithmetic and copies ran while one was open for 10% of the time, Pallas kernels for 0%

profile of v1, /device:TPU:0, one launch (start us, length us, event | category | flops | bytes accessed | tf_op | source)
XLA Modules:
  0.0 316.7 jit_solution(12454617680478117471)
XLA Ops:
  7.2 1.0 copy.18
  8.3 3.0 collective-permute-start
  11.3 3.1 collective-permute-start.1
  14.4 2.6 all_gather.19
  17.0 31.8 %all_gather.20 = bf16[384,768]{1,0:T(8,128)(2,1)S(1)} all-gather(bf16[48,768]{1,0:T(8,128)(2,1)} %param.13), channel_id=1, replica_groups=mesh['scene'=2,'tok'=8,'hid'=2] {'tok'}, dimensions={0}, use_global_device_ids=true | all-gather | bytes 663552 | tf_op jit(solution)/shard_map/all_gather | solution.py:58
  48.8 1.0 fusion.29
  49.8 31.5 %all_gather.18 = bf16[384,768]{1,0:T(8,128)(2,1)S(1)} all-gather(bf16[48,768]{1,0:T(8,128)(2,1)S(1)} %copy-done.15), channel_id=1, replica_groups=mesh['scene'=2,'tok'=8,'hid'=2] {'tok'}, dimensions={0}, use_global_device_ids=true | all-gather | bytes 663552 | tf_op jit(solution)/shard_map/all_gather | solution.py:56
  81.4 2.4 all_gather.21
  83.8 4.7 %collective-permute-start.3 = (bf16[48,768]{0,1:T(8,128)(2,1)S(1)}, bf16[48,768]{0,1:T(8,128)(2,1)}, u32[]{:S(2)}, u32[]{:S(2)}) collective-permute-start(bf16[48,768]{0,1:T(8,128)(2,1)S(1)} %collective-permute-done.1), channel_id=1, source_target_pairs={{0,14},{2,0},{4,2},{6,4},{8,6},{10,8},{12,10},{14,12},{1,15},{3,1}... | collective-permute-start | bytes 221192 | tf_op jit(solution)/shard_map/ppermute | solution.py:20
  88.5 1.4 collective-permute-done.2
  89.9 1.0 fusion.43
  90.9 2.0 collective-permute-done.3
  92.9 5.4 %collective-permute-start.5 = (bf16[48,768]{0,1:T(8,128)(2,1)}, bf16[48,768]{0,1:T(8,128)(2,1)}, u32[]{:S(2)}, u32[]{:S(2)}) collective-permute-start(bf16[48,768]{0,1:T(8,128)(2,1)} %collective-permute-done.3), channel_id=1, source_target_pairs={{0,14},{2,0},{4,2},{6,4},{8,6},{10,8},{12,10},{14,12},{1,15},{3,1}... | collective-permute-start | bytes 221192 | tf_op jit(solution)/shard_map/ppermute | solution.py:20
  98.3 2.2 fusion.15
  100.6 0.1 broadcast_in_dim.2
  100.6 2.0 dynamic_update_slice.24
  102.7 3.3 %dynamic_update_slice.25 = bf16[384,768]{0,1:T(8,128)(2,1)S(1)} dynamic-update-slice(bf16[384,768]{0,1:T(8,128)(2,1)S(1)} %dynamic_update_slice.24, bf16[48,768]{0,1:T(8,128)(2,1)} %copy-done.12, s32[]{:T(128)S(6)} %select_n.57, s32[]{:T(128)} %constant.77.clone.1) | dynamic-update-slice | bytes 147460 | tf_op jit(solution)/shard_map/dynamic_update_slice | solution.py:18
  106.0 3.5 %dynamic_update_slice.26 = bf16[384,768]{0,1:T(8,128)(2,1)S(1)} dynamic-update-slice(bf16[384,768]{0,1:T(8,128)(2,1)S(1)} %dynamic_update_slice.25, bf16[48,768]{0,1:T(8,128)(2,1)} %copy-done.13, s32[]{:T(128)S(6)} %select_n.59, s32[]{:T(128)} %constant.77.clone.1) | dynamic-update-slice | bytes 147460 | tf_op jit(solution)/shard_map/dynamic_update_slice | solution.py:21
  109.5 3.3 %dynamic_update_slice.27 = bf16[384,768]{0,1:T(8,128)(2,1)S(1)} dynamic-update-slice(bf16[384,768]{0,1:T(8,128)(2,1)S(1)} %dynamic_update_slice.26, bf16[48,768]{0,1:T(8,128)(2,1)} %copy-done.14, s32[]{:T(128)S(6)} %select_n.61, s32[]{:T(128)} %constant.77.clone.1) | dynamic-update-slice | bytes 147460 | tf_op jit(solution)/shard_map/dynamic_update_slice | solution.py:18
  112.8 3.5 %dynamic_update_slice.28 = bf16[384,768]{0,1:T(8,128)(2,1)S(1)} dynamic-update-slice(bf16[384,768]{0,1:T(8,128)(2,1)S(1)} %dynamic_update_slice.27, bf16[48,768]{0,1:T(8,128)(2,1)} %collective-permute-done.3, s32[]{:T(128)S(6)} %select_n.63, s32[]{:T(128)} %constant.77.clone.1) | dynamic-update-slice | bytes 147460 | tf_op jit(solution)/shard_map/dynamic_update_slice | solution.py:21
  116.4 3.5 %dynamic_update_slice.29 = bf16[384,768]{0,1:T(8,128)(2,1)S(1)} dynamic-update-slice(bf16[384,768]{0,1:T(8,128)(2,1)S(1)} %dynamic_update_slice.28, bf16[48,768]{0,1:T(8,128)(2,1)} %collective-permute-done.4, s32[]{:T(128)S(6)} %select_n.65, s32[]{:T(128)} %constant.77.clone.1) | dynamic-update-slice | bytes 147460 | tf_op jit(solution)/shard_map/dynamic_update_slice | solution.py:18
  119.9 3.5 %dynamic_update_slice.30 = bf16[384,768]{0,1:T(8,128)(2,1)S(1)} dynamic-update-slice(bf16[384,768]{0,1:T(8,128)(2,1)S(1)} %dynamic_update_slice.29, bf16[48,768]{0,1:T(8,128)(2,1)} %collective-permute-done.5, s32[]{:T(128)S(6)} %select_n.67, s32[]{:T(128)} %constant.77.clone.1) | dynamic-update-slice | bytes 147460 | tf_op jit(solution)/shard_map/dynamic_update_slice | solution.py:21
  123.5 3.5 %dynamic_update_slice.31 = bf16[384,768]{0,1:T(8,128)(2,1)S(1)} dynamic-update-slice(bf16[384,768]{0,1:T(8,128)(2,1)S(1)} %dynamic_update_slice.30, bf16[48,768]{0,1:T(8,128)(2,1)} %collective-permute-done.6, s32[]{:T(128)S(6)} %select_n.69, s32[]{:T(128)} %constant.77.clone.1) | dynamic-update-slice | bytes 147460 | tf_op jit(solution)/shard_map/dynamic_update_slice | solution.py:18
  127.0 1.0 fusion.42
  128.1 1.0 copy-done.3
  129.1 3.6 %fusion.9 = f32[384,768]{0,1:T(8,128)S(1)} fusion(bf16[1024,384]{0,1:T(8,128)(2,1)S(1)} %all_gather.21, f32[768,1024]{0,1:T(8,128)S(1)} %fusion.42, f32[1024,768]{1,0:T(8,128)} %copy-done.4, f32[1024,768]{1,0:T(8,128)S(1)} %copy-done.3), kind=kOutput, calls=%fused_computation.22 | convolution fusion | flops 612630528 | bytes 11403264 | tf_op jit(solution)/shard_map/dot_general | solution.py:33
  132.8 1.3 fusion.12
  134.1 2.1 pad_maximum_fusion
  136.2 0.0 reduce-scatter.5.cloned.1.call-start
  136.3 1.1 copy.17
  137.3 1.1 copy.23
  138.4 2.0 all_gather.23
  140.4 2.2 all_gather.22
  142.6 134.2 %all-reduce.3.cloned.1.call-done = f32[384,2304]{0,1:T(8,128)} async-done(((f32[384,2304]{0,1:T(8,128)}), f32[384,2304]{0,1:T(8,128)}) %all-reduce.3.cloned.1.call-update) | async-done | bytes 3538960 | tf_op jit(solution)/shard_map/psum | solution.py:69
  276.9 4.1 %multiply_reduce_fusion.2 = (f32[384]{0:T(512)S(1)}, f32[384]{0:T(512)S(1)}, f32[384]{0:T(512)S(1)}, f32[384]{0:T(512)S(1)}, f32[384]{0:T(512)}, /*index=5*/f32[...) fusion(f32[384,2304]{0,1:T(8,128)} %all-reduce.3.cloned.1.call-done, bf16[384,768]{0,1:T(8,128)(2,1)} %copy.17, ...), kind=kLoop, calls=%fused_computation.42 | loop fusion | flops 6189696 | bytes 5322240 | tf_op jit(solution)/shard_map/reduce_sum | solution.py:88
  280.9 4.6 %all-reduce = (f32[384]{0:T(512)}, f32[384]{0:T(512)}, f32[384]{0:T(512)}, f32[384]{0:T(512)}, f32[384]{0:T(512)}, /*index=5*/f32[384]{0:T(512)}, f32[384]{0:T(512)}, f32[384]{0:T(512)}, f32[384]{0:T(512)}) all-reduce(f32[384]{0:T(512)S(1)} %get-tuple-element.5, ...), channel_id=1, replica_groups=mesh['scene'=2,'tok'=8,'hid'=2] {'hid'}, use_global_device_ids=true, to_apply=%region_18.19 | all-reduce | flops 3456 | bytes 27648 | tf_op jit(solution)/shard_map/psum | solution.py:89
  285.5 0.7 rsqrt_multiply_fusion.5
  286.3 0.7 rsqrt_multiply_fusion.1
  287.0 2.0 fusion.18
  289.1 0.3 convolution_bitcast_fusion.1
  289.4 0.3 convolution_bitcast_fusion.2
  289.7 0.3 copy-done.10
  290.1 0.3 convolution_bitcast_fusion
  290.4 0.5 fusion.33
  290.9 1.1 fusion.28
  292.0 1.0 convolution_convert_fusion
  293.1 5.6 %reduce-scatter.5.cloned.1.call-done = bf16[128,192]{0,1:T(8,128)(2,1)} async-done(((bf16[128,384]{0,1:T(8,128)(2,1)}), bf16[128,192]{0,1:T(8,128)(2,1)}) %reduce-scatter.5.cloned.1.call-update) | async-done | bytes 49168 | tf_op jit(solution)/shard_map/reduce_scatter | solution.py:119
  298.7 11.5 %reduce-scatter.3.cloned.1.call-done = bf16[128,192]{0,1:T(8,128)(2,1)} async-done(((bf16[128,384]{0,1:T(8,128)(2,1)}), bf16[128,192]{0,1:T(8,128)(2,1)}) %reduce-scatter.3.cloned.1.call-update) | async-done | bytes 49168 | tf_op jit(solution)/shard_map/reduce_scatter | solution.py:116
  (49 shorter events, 0.2 us)
Async XLA Ops:
  7.2 41.6 %copy-start.18 = (f32[1024]{0:T(1024)S(1)}, f32[1024]{0:T(1024)}, u32[]{:S(2)}) copy-start(f32[1024]{0:T(1024)} %param.10) | copy-start | bytes 12292
  7.2 269.7 %all-reduce.3.cloned.1.call-start = ((), (), s32[]{:S(2)}) async-start(), calls=%async_computation.2 | async-start | bytes 7077888 | tf_op jit(solution)/shard_map/psum | solution.py:69
  8.3 73.1 %collective-permute-start = (bf16[48,768]{0,1:T(8,128)(2,1)S(1)}, bf16[48,768]{0,1:T(8,128)(2,1)S(1)}, u32[]{:S(2)}, u32[]{:S(2)}) collective-permute-start(bf16[48,768]{0,1:T(8,128)(2,1)S(1)} %copy.18), channel_id=1, source_target_pairs={{0,2},{2,4},{4,6},{6,8},{8,10},{10,12},{12,14},{14,0},{1,3},{3,5},... | collective-permute-start | bytes 221192 | tf_op jit(solution)/shard_map/ppermute | solution.py:17
  11.3 72.5 %collective-permute-start.1 = (bf16[48,768]{0,1:T(8,128)(2,1)S(1)}, bf16[48,768]{0,1:T(8,128)(2,1)S(1)}, u32[]{:S(2)}, u32[]{:S(2)}) collective-permute-start(bf16[48,768]{0,1:T(8,128)(2,1)S(1)} %copy.18), channel_id=1, source_target_pairs={{0,14},{2,0},{4,2},{6,4},{8,6},{10,8},{12,10},{14,12},{1,15},{3,1}... | collective-permute-start | bytes 221192 | tf_op jit(solution)/shard_map/ppermute | solution.py:20
  48.8 1.0 copy-start.15
  48.8 32.6 %copy-start.11 = (bf16[1024,192]{0,1:T(8,128)(2,1)S(1)}, bf16[1024,192]{0,1:T(8,128)(2,1)}, u32[]{:S(2)}) copy-start(bf16[1024,192]{0,1:T(8,128)(2,1)} %param.8) | copy-start | bytes 1179652
  49.8 48.5 %copy-start.2 = (f32[1024,768]{1,0:T(8,128)}, f32[1024,768]{1,0:T(8,128)S(1)}, u32[]{:S(2)}) copy-start(f32[1024,768]{1,0:T(8,128)S(1)} %fusion.29) | copy-start | bytes 9437188
  81.4 9.5 %copy-start.12 = (bf16[48,768]{0,1:T(8,128)(2,1)}, bf16[48,768]{0,1:T(8,128)(2,1)S(1)}, u32[]{:S(2)}) copy-start(bf16[48,768]{0,1:T(8,128)(2,1)S(1)} %collective-permute-done) | copy-start | bytes 221188
  81.4 8.5 %collective-permute-start.2 = (bf16[48,768]{0,1:T(8,128)(2,1)S(1)}, bf16[48,768]{0,1:T(8,128)(2,1)S(1)}, u32[]{:S(2)}, u32[]{:S(2)}) collective-permute-start(bf16[48,768]{0,1:T(8,128)(2,1)S(1)} %collective-permute-done), channel_id=1, source_target_pairs={{0,2},{2,4},{4,6},{6,8},{8,10},{10,12},{12,14},{14,0},{1,3},{3,5},... | collective-permute-start | bytes 221192 | tf_op jit(solution)/shard_map/ppermute | solution.py:17
  83.8 7.1 %copy-start.13 = (bf16[48,768]{0,1:T(8,128)(2,1)}, bf16[48,768]{0,1:T(8,128)(2,1)S(1)}, u32[]{:S(2)}) copy-start(bf16[48,768]{0,1:T(8,128)(2,1)S(1)} %collective-permute-done.1) | copy-start | bytes 221188
  83.8 9.2 %collective-permute-start.3 = (bf16[48,768]{0,1:T(8,128)(2,1)S(1)}, bf16[48,768]{0,1:T(8,128)(2,1)}, u32[]{:S(2)}, u32[]{:S(2)}) collective-permute-start(bf16[48,768]{0,1:T(8,128)(2,1)S(1)} %collective-permute-done.1), channel_id=1, source_target_pairs={{0,14},{2,0},{4,2},{6,4},{8,6},{10,8},{12,10},{14,12},{1,15},{3,1}... | collective-permute-start | bytes 221192 | tf_op jit(solution)/shard_map/ppermute | solution.py:20
  89.8 1.0 copy-start.14
  89.8 8.5 %collective-permute-start.4 = (bf16[48,768]{0,1:T(8,128)(2,1)S(1)}, bf16[48,768]{0,1:T(8,128)(2,1)}, u32[]{:S(2)}, u32[]{:S(2)}) collective-permute-start(bf16[48,768]{0,1:T(8,128)(2,1)S(1)} %collective-permute-done.2), channel_id=1, source_target_pairs={{0,2},{2,4},{4,6},{6,8},{8,10},{10,12},{12,14},{14,0},{1,3},{3,5},... | collective-permute-start | bytes 221192 | tf_op jit(solution)/shard_map/ppermute | solution.py:17
  90.9 9.7 %copy-start.4 = (f32[1024,768]{1,0:T(8,128)}, f32[1024,768]{1,0:T(8,128)S(1)}, u32[]{:S(2)}) copy-start(f32[1024,768]{1,0:T(8,128)S(1)} %fusion.43) | copy-start | bytes 9437188
  92.9 27.0 %collective-permute-start.5 = (bf16[48,768]{0,1:T(8,128)(2,1)}, bf16[48,768]{0,1:T(8,128)(2,1)}, u32[]{:S(2)}, u32[]{:S(2)}) collective-permute-start(bf16[48,768]{0,1:T(8,128)(2,1)} %collective-permute-done.3), channel_id=1, source_target_pairs={{0,14},{2,0},{4,2},{6,4},{8,6},{10,8},{12,10},{14,12},{1,15},{3,1}... | collective-permute-start | bytes 221192 | tf_op jit(solution)/shard_map/ppermute | solution.py:20
  98.3 25.1 %collective-permute-start.6 = (bf16[48,768]{0,1:T(8,128)(2,1)}, bf16[48,768]{0,1:T(8,128)(2,1)}, u32[]{:S(2)}, u32[]{:S(2)}) collective-permute-start(bf16[48,768]{0,1:T(8,128)(2,1)} %collective-permute-done.4), channel_id=1, source_target_pairs={{0,2},{2,4},{4,6},{6,8},{8,10},{10,12},{12,14},{14,0},{1,3},{3,5},... | collective-permute-start | bytes 221192 | tf_op jit(solution)/shard_map/ppermute | solution.py:17
  127.0 1.1 copy-start.1
  127.0 2.1 copy-start.3
  129.1 3.6 %copy-start.5 = (f32[1024,768]{1,0:T(8,128)S(1)}, f32[1024,768]{1,0:T(8,128)}, u32[]{:S(2)}) copy-start(f32[1024,768]{1,0:T(8,128)} %copy-done.4) | copy-start | bytes 9437188
  132.7 1.4 copy-start.8
  136.2 2.2 copy-start.16
  136.2 4.2 %copy-start.17 = (bf16[128,192]{0,1:T(8,128)(2,1)S(1)}, bf16[128,192]{0,1:T(8,128)(2,1)}, u32[]{:S(2)}) copy-start(bf16[128,192]{0,1:T(8,128)(2,1)} %param.14) | copy-start | bytes 147460
  136.2 162.5 %reduce-scatter.5.cloned.1.call-start = ((), (), s32[]{:S(2)}) async-start(), calls=%async_computation.4 | async-start | bytes 147456 | tf_op jit(solution)/shard_map/reduce_scatter | solution.py:119
  276.9 10.1 %copy-start = (f32[384,2304]{0,1:T(8,128)S(1)}, f32[384,2304]{0,1:T(8,128)}, u32[]{:S(2)}) copy-start(f32[384,2304]{0,1:T(8,128)} %all-reduce.3.cloned.1.call-done) | copy-start | bytes 10616836
  287.0 2.1 copy-start.9
  289.1 1.3 copy-start.6
  289.1 1.0 copy-start.10
  290.9 1.1 copy-start.7
  291.9 18.2 %reduce-scatter.3.cloned.1.call-start = ((), (), s32[]{:S(2)}) async-start(), calls=%async_computation.3 | async-start | bytes 147456 | tf_op jit(solution)/shard_map/reduce_scatter | solution.py:116
Sparse Core Ops, SparseCore 0:
  136.3 140.4 all-reduce.2
  292.1 6.5 reduce-scatter.4
  301.5 8.6 reduce-scatter.2
